TPU v7x, 32 devices: a whole 2x2x4 slice. The times are simulated.
32 devices in a mesh: pair: 8 (over z, y), band: 4 (over x, core).
Axes of the slice: x: 2, y: 2, z: 4, core: 2. Of those that a mesh axis runs over, the one named last changes fastest.
Arguments:
- orbitals: bfloat16 [2048, 23, 64], P('pair'), may hold values from -6 to 6
- screening: bfloat16 [1024, 8, 1024], P('pair', None, 'band'), may hold values from -0.1875 to 0.1875
- trial: bfloat16 [1024, 23, 64], P('pair'), may hold values from -6 to 6
- pair_kpts: int32 [8, 2], replicated, may hold values from 0 to 22
- pair_q: int32 [8], replicated, may hold values from 0 to 7
Outputs:
- applied: float32 [1024, 23, 64], P('pair', None, 'band')
All inputs are finite; a program needn't handle non-finite values.
Results may differ from a plain program's by a relative error of at most 0.013.
Values may be sent and summed in bfloat16 or wider, within the bound.
No kernel may reach another device: no remote copies, remote signals or barrier semaphores. Data moves between devices by JAX's collectives and lax.ppermute only.
A program may use at most 64 MiB of HBM per device.

v0:
```python
import math

import jax
import jax.numpy as jnp
from jax import lax
from jax.experimental import pallas as pl
from jax.experimental.pallas import tpu as pltpu
from jax.sharding import Mesh, PartitionSpec as P


NV = 32
NC = 32
NR = 2048
NG = 1024
NVC = NV * NC
LANES = 128
HALVES = 2
TABLE = 32
F32 = jnp.float32
BF16 = jnp.bfloat16
VMEM_LIMIT = 40 * 1024 * 1024


def dot(a, b):
    return lax.dot_general(a, b, (((1,), (0,)), ((), ())), preferred_element_type=F32)


def dot_rows(a, b):
    return lax.dot_general(a, b, (((1,), (1,)), ((), ())), preferred_element_type=F32)


SPACES = {"s": pltpu.SMEM, "v": pltpu.VMEM, "h": pl.ANY}


def call(body, inputs, outputs, scratch=(), flops=0, aliases=None):
    specs, arrays = [], []
    for space, array in inputs:
        specs.append(pl.BlockSpec(memory_space=SPACES.get(space, pltpu.VMEM)))
        home = pltpu.VMEM if space == "v" else pltpu.HBM
        array = pltpu.with_memory_space_constraint(array, home)
        arrays.append(array)
    shapes, out_specs = [], []
    for space, shape, dtype in outputs:
        kind = {"v": pltpu.VMEM, "h": pltpu.HBM}.get(space, jax.ShapeDtypeStruct)
        shapes.append(kind(shape, dtype))
        out_specs.append(pl.BlockSpec(memory_space=SPACES.get(space, pltpu.VMEM)))
    return pl.pallas_call(
        body,
        out_shape=shapes,
        in_specs=specs,
        out_specs=out_specs,
        scratch_shapes=list(scratch),
        input_output_aliases=aliases or {},
        compiler_params=pltpu.CompilerParams(vmem_limit_bytes=VMEM_LIMIT),
        cost_estimate=pl.CostEstimate(flops=int(flops), transcendentals=0, bytes_accessed=1 << 20),
    )(*arrays)


def pack_kernel(kpts_ref, q_ref, orbital_ref, trial_ref, screen_ref, out_ref, *refs):
    *sends, room, table, ordered, fetch_sems, send_sems, table_sem = refs
    bx, bc = lax.axis_index("bx"), lax.axis_index("bc")
    strips, low = lax.axis_size("bx"), room.shape[0]
    points = orbital_ref.shape[2]
    bands = pl.ds(pl.multiple_of(bc * NV, NV), NV)
    fetches = []
    for d in range(low):
        pair = d * strips + bx
        first, second, own = kpts_ref[0, pair], kpts_ref[1, pair], kpts_ref[bc, pair]
        parts = (
            (orbital_ref.at[first, bands, :], room.at[d, pl.ds(0, NV), pl.ds(0, points)]),
            (orbital_ref.at[second, bands, :], room.at[d, pl.ds(NV, NV), pl.ds(0, points)]),
            (trial_ref.at[own], room.at[d, :, pl.ds(points, trial_ref.shape[2])]),
        )
        fetches.append([pltpu.make_async_copy(x, y, fetch_sems.at[d, k]) for k, (x, y) in enumerate(parts)])
        for fetch in fetches[-1]:
            fetch.start()
    table_fetch = pltpu.make_async_copy(screen_ref, table, table_sem)
    table_fetch.start()
    copies = []
    for d in range(low):
        for fetch in fetches[d]:
            fetch.wait()
        for h in range(out_ref.shape[0] // low):
            copies.append(pltpu.make_async_copy(room.at[d], out_ref.at[h * low + d], send_sems.at[h, d]))
            copies[-1].start()
    table_fetch.wait()
    me = lax.axis_index(("pl", "bx"))
    rows, columns = sends[0].shape
    kinds = screen_ref.shape[0] // rows
    source = lax.broadcasted_iota(jnp.int32, (columns, columns), 0)
    target = lax.broadcasted_iota(jnp.int32, (columns, columns), 1)
    wanted = target % (columns // 2) * 2 + target // (columns // 2)
    order = jnp.where(source == wanted, 1.0, 0.0).astype(BF16)
    result = dot(table[...], order)
    for t in range(columns // LANES):
        ordered[t] = result[:, t * LANES : (t + 1) * LANES]
    for distance, send in zip(distances(len(sends)), sends):
        q = q_ref[me ^ own_distance(distance)]
        for odd in range(2):
            for t in range(columns // LANES):
                send[odd * rows // 2 : (odd + 1) * rows // 2, t * LANES : (t + 1) * LANES] = ordered[
                    t, pl.ds(q + kinds * odd, rows // 2, stride=2 * kinds), :
                ].astype(BF16)
    for copy in copies:
        copy.wait()


def basis_kernel(rows, cos_low, sin_low, cos_high, sin_high):
    columns = rows.shape[1]
    quarter = columns // 4
    groups = lax.axis_size("bc")
    strip = NG // (lax.axis_size("bx") * groups)
    column = lax.broadcasted_iota(jnp.int32, (1, columns), 1)
    odd = column // quarter % 2
    inner = column % quarter
    frequency = jnp.where(
        column < 2 * quarter,
        lax.axis_index("ph") * 2 * quarter + 2 * inner,
        (inner // (strip // 2) * groups + lax.axis_index("bc")) * strip + 2 * (inner % (strip // 2)),
    ) + odd
    period = 4 * NR
    unit = math.pi / (2 * NR)
    fine = 8

    def turn(count, step, offset):
        multiple = lax.broadcasted_iota(jnp.int32, (count, columns), 0) * step + offset
        index = multiple * frequency & (period - 1)
        angle = jnp.where(index >= period // 2, index - period, index).astype(F32) * unit
        return jnp.cos(angle), jnp.sin(angle)

    def table(step, offset, cos_ref, sin_ref, scale):
        cos_a, sin_a = turn(fine, step, offset)
        cos_b, sin_b = turn(TABLE // fine, step * fine, 0)
        cos_a, sin_a = cos_a * scale, sin_a * scale
        for k in range(TABLE // fine):
            c, s = cos_b[k : k + 1], sin_b[k : k + 1]
            cos_ref[k * fine : (k + 1) * fine, :] = cos_a * c - sin_a * s
            sin_ref[k * fine : (k + 1) * fine, :] = sin_a * c + cos_a * s

    table(2, 1, cos_low, sin_low, math.sqrt(2.0 / NR))
    table(2 * TABLE, 0, cos_high, sin_high, 1.0)

    def step(block, carry):
        high = pl.ds(block, 1)
        value = cos_low[...] * cos_high[high, :] - sin_low[...] * sin_high[high, :]
        rows[pl.ds(pl.multiple_of(block * TABLE, TABLE), TABLE), :] = value.astype(BF16)
        return carry

    lax.fori_loop(0, rows.shape[0] // TABLE, step, 0)


def distances(count):
    order = [0] + [d for d in (1, 7, 5, 3, 6, 4, 2) if d < count]
    order += [d for d in range(1, count) if d not in order]
    return [(d, (d << 1) % count | (d << 1) // count) for d in order]


def own_distance(pair):
    return jnp.where(lax.axis_index("bc") % 2 == 0, pair[0], pair[1])


def waves_kernel(own_ref, other_ref, _, waves_ref, first, second, even, odd):
    side = lax.axis_index("bc")
    blocks, _, _ = own_ref.shape
    points = NR // blocks
    piece = 256 if points % 256 == 0 else LANES
    middle = NR // 2
    quarter = waves_ref.shape[1] // 4
    source = lax.broadcasted_iota(jnp.int32, (piece, piece), 0)
    target = lax.broadcasted_iota(jnp.int32, (piece, piece), 1)
    flip = jnp.where(source + target == piece - 1, 1.0, 0.0).astype(BF16)
    for slot, ref in ((side, own_ref), (1 - side, other_ref)):
        for start in range(0, middle, piece):
            ahead = ref[start // points, :, start % points : start % points + piece].astype(F32)
            mirror = NR - start - piece
            behind = dot(ref[mirror // points, :, mirror % points : mirror % points + piece], flip)
            for half_of, value in enumerate((ahead, behind)):
                first[slot, half_of, :, start : start + piece] = value[:NV]
                second[slot, half_of, :, start : start + piece] = value[NV:]

    for kind in (1, 0):
        outer, inner = (second, first) if kind else (first, second)
        for v in range(NV):
            rows = slice(v * NV, (v + 1) * NV)
            ahead = outer[kind, 0, v : v + 1, :] * inner[kind, 0]
            behind = outer[kind, 1, v : v + 1, :] * inner[kind, 1]
            even[kind, rows, :] = (ahead + behind).astype(BF16)
            odd[kind, rows, :] = (ahead - behind).astype(BF16)
        spans = [slice((2 * kind + parity) * quarter, (2 * kind + parity + 1) * quarter) for parity in range(2)]
        results = [dot(x[kind], waves_ref[:, span]).astype(BF16) for x, span in zip((even, odd), spans)]
        for span, result in zip(spans, results):
            waves_ref[:, span] = result


def pair_kernel(own_ref, other_ref, waves_ref, *refs):
    *screens, keep_ref, give_ref, conduction, screen, screened = refs[:-5]
    slabs, vectors, diagonal, sides, shares = refs[-5:]
    side = lax.axis_index("bc")
    blocks, count, width = own_ref.shape
    states = NVC // blocks
    half = screened.shape[1]
    quarter = half // 2
    strips = lax.axis_size("bx")
    run = quarter // strips
    broad = screen.shape[2]
    for parity in range(2):
        for s in range(strips):
            source, target = half + parity * quarter + s * run, (2 * s + parity) * run
            conduction[:, target : target + run] = waves_ref[:, source : source + run]
    if len(screens) > 1:
        me = lax.axis_index(("pl", "bx"))
        part = screens[0].shape[0] // 2
        for distance, ref in zip(distances(len(screens)), screens):
            origin = me ^ own_distance(distance)
            for parity in range(2):
                at = pl.multiple_of(parity * quarter + origin // strips * part, part)
                screen[origin % strips, pl.ds(at, part), :] = ref[parity * part : (parity + 1) * part, :]
    else:
        screen[...] = screens[0][...]

    repeat = LANES // NV
    lanes = repeat * count
    fold = LANES // count
    lane = lax.broadcasted_iota(jnp.int32, (NV, lanes), 1) // count
    masks = [jnp.where(lane == r, 1.0, 0.0).astype(BF16) for r in range(repeat)]
    for b in range(blocks):
        for slot, ref in ((side, own_ref), (1 - side, other_ref)):
            turned = ref[b, :, width - states :].astype(F32).T
            vectors[slot, b * states : (b + 1) * states, :] = jnp.concatenate([turned] * fold, axis=1)
    for kind in range(2):
        for j in range(NC):
            rows = vectors[1, pl.ds(j, NV, stride=NV), :] if kind == 0 else vectors[0, j * NC : (j + 1) * NC, :]
            rows = jnp.concatenate([rows.astype(BF16)] * (lanes // LANES), axis=1)
            for r in range(repeat):
                diagonal[kind, j * LANES + r * NV : j * LANES + (r + 1) * NV, :] = rows * masks[r]

    for s in range(strips):
        screened[:, s * broad : (s + 1) * broad] = dot(waves_ref[:, :half], screen[s]).astype(BF16)

    groups = NVC // LANES
    scale = 1.0 / math.sqrt(NVC) / math.sqrt(NG)
    source = lax.broadcasted_iota(jnp.int32, (LANES, LANES), 0)
    target = lax.broadcasted_iota(jnp.int32, (LANES, LANES), 1)
    weave = jnp.where(target == source % NV * repeat + source // NV, 1.0, 0.0).astype(BF16)

    cores, _, _, share, places = shares.shape

    def put(kind, i, value):
        to, at = i * LANES // places, i * LANES % places
        for b in range(count // share):
            strip, core = b // cores, b % cores
            shares[core, to * strips + strip, kind, :, at : at + LANES] = value[b * share : (b + 1) * share]

    for kind in range(2):
        raw = dot_rows(conduction[...], screened[...]).astype(BF16) if kind == 0 else raw.T
        for j in range(NC):
            for g in range(groups):
                slabs[kind, g * NC : (g + 1) * NC, j * LANES : (j + 1) * LANES] = raw[
                    j * NC : (j + 1) * NC, g * LANES : (g + 1) * LANES
                ]
        total = dot(slabs[kind], diagonal[kind]) * scale
        if kind == 0:
            for g in range(groups):
                block = total[g * NC : (g + 1) * NC, :]
                stacked = jnp.concatenate([block[:, r * count : (r + 1) * count] for r in range(repeat)], axis=0)
                put(0, g, stacked.T.astype(BF16))
            continue
        for t in range(lanes // LANES):
            sides[t] = total[:, t * LANES : (t + 1) * LANES]
        for at in range(0, groups, fold):
            strands = []
            for r in range(repeat):
                for w in range(repeat):
                    pieces = [
                        sides[r // fold, pl.ds((at + f) * repeat + w, groups, stride=NV), :][
                            :, r % fold * count : (r % fold + 1) * count
                        ]
                        for f in range(fold)
                    ]
                    strands.append(jnp.concatenate(pieces, axis=1))
            stacked = jnp.concatenate(strands, axis=0).astype(BF16)
            woven = lax.dot_general(stacked, weave, (((0,), (0,)), ((), ())), preferred_element_type=F32)
            for f in range(fold):
                put(1, at + f, woven[f * count : (f + 1) * count].astype(BF16))
    keep_ref[...] = shares[side]
    give_ref[...] = shares[1 - side]


def add_kernel(one_ref, other_ref, out_ref):
    out_ref[...] = (one_ref[...].astype(F32) + other_ref[...].astype(F32)).astype(BF16)


def gather_kernel(kpts_ref, got_ref, out_ref):
    out_ref[...] = jnp.zeros_like(out_ref)
    halves, low, strips = got_ref.shape[:3]
    for p in range(low * strips):
        for s in range(2):
            total = got_ref[0, p // strips, p % strips, s].astype(F32)
            for h in range(1, halves):
                total += got_ref[h, p // strips, p % strips, s].astype(F32)
            out_ref[kpts_ref[s, p]] += total


def on_device(orbitals, screening, trial, pair_kpts, pair_q):
    halves, low, strips, groups = (lax.axis_size(a) for a in ("ph", "pl", "bx", "bc"))
    pair_axes = ("ph", "pl")
    pair_count = halves * low
    points, kpt_count, _ = orbitals.shape
    states, _, count = trial.shape
    tall, kinds, broad = screening.shape
    half = NG // HALVES
    aligned = points % LANES == 0 and states % LANES == 0 and pair_count & (pair_count - 1) == 0
    orbital_t, trial_t = orbitals.transpose(1, 2, 0), trial.transpose(1, 2, 0)
    kpts_t = pair_kpts.T

    if aligned:
        send, *screen_sends = call(
            pack_kernel,
            [
                ("s", kpts_t),
                ("s", pair_q),
                ("h", orbital_t),
                ("h", trial_t),
                ("h", screening.reshape(tall * kinds, broad)),
            ],
            [("h", (pair_count, count, points + states), BF16)] + [("b", (tall, broad), BF16)] * (low * strips),
            [
                pltpu.VMEM((low, count, points + states), BF16),
                pltpu.VMEM((tall * kinds, broad), BF16),
                pltpu.VMEM((broad // LANES, tall * kinds, LANES), F32),
                pltpu.SemaphoreType.DMA((low, 3)),
                pltpu.SemaphoreType.DMA((halves, low)),
                pltpu.SemaphoreType.DMA,
            ],
            flops=NG * NG * 256,
        )
    else:
        bx, bc = lax.axis_index("bx"), lax.axis_index("bc")
        near = lax.dynamic_index_in_dim(pair_kpts.reshape(low, strips, 2), bx, 1, keepdims=False)
        orbital_half = lax.dynamic_slice_in_dim(orbital_t, bc * NV, NV, 1)
        orbital_part = orbital_half[near].reshape(low, 2 * NV, points)
        trial_part = trial_t[lax.dynamic_index_in_dim(near, bc, 1, keepdims=False)]
        send = jnp.concatenate([orbital_part, trial_part], axis=2)
        send = jnp.concatenate([send] * halves, axis=0)
        screen_send = screening.transpose(1, 0, 2)[pair_q]
    got = lax.all_to_all(send, pair_axes, split_axis=0, concat_axis=0, tiled=True)
    basis = call(
        basis_kernel,
        [],
        [("v", (NR // 2, 2 * half), BF16)],
        [pltpu.VMEM((TABLE, 2 * half), F32)] * 4,
        flops=NR * NG * 8,
    )[0]
    if aligned:
        screens = list(screen_sends[:1])
        for step, distance in list(enumerate(distances(low * strips)))[1:]:
            to = [
                (i * groups + g, (i ^ distance[g % 2]) * groups + g) for i in range(low * strips) for g in range(groups)
            ]
            screens.append(lax.ppermute(screen_sends[step], ("pl", "bx", "bc"), to))
    else:
        screen_got = lax.all_to_all(screen_send, ("pl", "bx"), split_axis=0, concat_axis=0, tiled=True)
    other = lax.ppermute(got, "bc", [(i, i ^ 1) for i in range(groups)])

    if not aligned:

        def joined(x):
            turned = x.transpose(1, 0, 2)
            return jnp.concatenate(
                [turned[:, :, :points].reshape(1, count, NR), turned[:, :, points:].reshape(1, count, NVC)], axis=2
            )

        got, other = joined(got), joined(other)
        screen_got = screen_got.reshape(low, strips, tall // 2, 2, broad // 2, 2).transpose(1, 3, 0, 2, 5, 4)
        screens = [screen_got.reshape(strips, low * tall, broad)]

    share = count // (strips * groups)
    lanes = LANES // NV * count
    places = states if aligned else NVC
    shape = (NVC // places * strips, 2, share, places)
    waves = call(
        waves_kernel,
        [("v", got), ("v", other), ("v", basis)],
        [("v", (NR // 2, 2 * half), BF16)],
        [pltpu.VMEM((2, 2, NV, NR // 2), F32)] * 2 + [pltpu.VMEM((2, NVC, NR // 2), BF16)] * 2,
        flops=2 * NVC * NR * half,
        aliases={2: 0},
    )[0]
    keep, give = call(
        pair_kernel,
        [("v", got), ("v", other), ("v", waves)] + [("v", x) for x in screens],
        [("v", shape, BF16)] * 2,
        [
            pltpu.VMEM((NVC, half), BF16),
            pltpu.VMEM((strips, half, broad), BF16),
            pltpu.VMEM((NVC, half), BF16),
            pltpu.VMEM((2, NVC // LANES * NC, NC * LANES), BF16),
            pltpu.VMEM((2, NVC, LANES), F32),
            pltpu.VMEM((2, NC * LANES, lanes), BF16),
            pltpu.VMEM((lanes // LANES, NVC // LANES * NC, LANES), F32),
            pltpu.VMEM((groups,) + shape, BF16),
        ],
        flops=2 * NVC * half * half + 8 * NVC * NVC * half,
    )
    taken = lax.ppermute(give, "bc", [(i, i ^ 1) for i in range(groups)])
    partial = call(add_kernel, [("v", keep), ("v", taken)], [("v", shape, BF16)])[0]
    if not aligned:
        partial = partial.reshape(strips, 2, share, pair_count, states).transpose(3, 0, 1, 2, 4)
        partial = partial.reshape(pair_count * strips, 2, share, states)
    out_got = lax.all_to_all(partial, ("ph", "pl", "bx"), split_axis=0, concat_axis=0, tiled=True)
    out_got = out_got.reshape(halves, low, strips, 2, share, states)
    if aligned:
        applied = call(gather_kernel, [("s", kpts_t), ("v", out_got)], [("b", (kpt_count, share, states), F32)])[0]
    else:
        summed = jnp.sum(out_got.astype(F32), axis=0).reshape(-1, share * states)
        hot = (pair_kpts.reshape(-1)[None, :] == jnp.arange(kpt_count)[:, None]).astype(F32)
        applied = lax.dot_general(
            hot, summed, (((1,), (0,)), ((), ())), precision=lax.Precision.HIGHEST, preferred_element_type=F32
        ).reshape(kpt_count, share, states)
    return applied.transpose(2, 0, 1)


def solution(mesh):
    pair_count, band_count = mesh.shape["pair"], mesh.shape["band"]
    shape = (HALVES, pair_count // HALVES, 2, band_count // 2)
    fine = Mesh(mesh.devices.reshape(shape), ("ph", "pl", "bx", "bc"))
    pair_axes, band_axes = ("ph", "pl"), ("bx", "bc")
    return jax.shard_map(
        on_device,
        mesh=fine,
        in_specs=(
            P(pair_axes, None, None),
            P(pair_axes, None, band_axes),
            P(pair_axes, None, None),
            P(),
            P(),
        ),
        out_specs=P(pair_axes, None, band_axes),
        check_vma=False,
    )
```

profile of v0, /device:TPU:0, one launch (start us, length us, event | category | flops | bytes accessed | tf_op | source)
XLA Modules:
  0.0 54.6 jit_solution(8408517630352252696)
XLA Ops:
  0.0 2.8 %shard_map.55 = (bf16[8,64,384]{2,1,0:T(8,128)(2,1)}, bf16[128,256]{1,0:T(8,128)(2,1)S(1)}, bf16[128,256]{1,0:T(8,128)(2,1)S(1)}, bf16[128,256]{1,0:T(8,128)(2,1...) custom-call(s32[2,8]{1,0:T(2,128)} %bitcast.10, ...), custom_call_target="tpu_custom_call" | custom-call | flops 268435456 | bytes 1048576 | tf_op jit(solution)/shard_map/pallas_call | solution.py:47
  2.8 19.4 %all_to_all.10.own_ref = bf16[8,64,384]{2,1,0:T(8,128)(2,1)S(1)} all-to-all(bf16[8,64,384]{2,1,0:T(8,128)(2,1)} %get-tuple-element.16), channel_id=1, replica_groups=mesh['ph'=2,'pl'=4,'bx'=2,'bc'=2] {'ph','pl'}, dimensions={0} | all-to-all | bytes 786432 | tf_op jit(solution)/shard_map/all_to_all | solution.py:346
  22.2 0.0 collective-permute-start
  22.2 1.5 %collective-permute-start.1 = (bf16[128,256]{1,0:T(8,128)(2,1)S(1)}, bf16[128,256]{1,0:T(8,128)(2,1)S(1)}, u32[]{:S(2)}, u32[]{:S(2)}) collective-permute-start(bf16[128,256]{1,0:T(8,128)(2,1)S(1)} %get-tuple-element.18), channel_id=1, source_target_pairs={{0,2},{1,5},{2,0},{3,7},{4,6},{5,1},{6,4},{7,3},{8,10},{9,13},{10,... | collective-permute-start | bytes 196616 | tf_op jit(solution)/shard_map/ppermute | solution.py:360
  23.7 0.7 %collective-permute-start.2 = (bf16[128,256]{1,0:T(8,128)(2,1)S(1)}, bf16[128,256]{1,0:T(8,128)(2,1)S(1)}, u32[]{:S(2)}, u32[]{:S(2)}) collective-permute-start(bf16[128,256]{1,0:T(8,128)(2,1)S(1)} %get-tuple-element.19), channel_id=1, source_target_pairs={{0,14},{1,15},{2,12},{3,13},{4,10},{5,11},{6,8},{7,9},{8,6},{9,7},... | collective-permute-start | bytes 196616 | tf_op jit(solution)/shard_map/ppermute | solution.py:360
  24.4 2.7 %collective-permute-start.3 = (bf16[128,256]{1,0:T(8,128)(2,1)S(1)}, bf16[128,256]{1,0:T(8,128)(2,1)S(1)}, u32[]{:S(2)}, u32[]{:S(2)}) collective-permute-start(bf16[128,256]{1,0:T(8,128)(2,1)S(1)} %get-tuple-element.20), channel_id=1, source_target_pairs={{0,10},{1,7},{2,8},{3,5},{4,14},{5,3},{6,12},{7,1},{8,2},{9,15},{1... | collective-permute-start | bytes 196616 | tf_op jit(solution)/shard_map/ppermute | solution.py:360
  27.1 0.9 %collective-permute-start.4 = (bf16[128,256]{1,0:T(8,128)(2,1)S(1)}, bf16[128,256]{1,0:T(8,128)(2,1)S(1)}, u32[]{:S(2)}, u32[]{:S(2)}) collective-permute-start(bf16[128,256]{1,0:T(8,128)(2,1)S(1)} %get-tuple-element.21), channel_id=1, source_target_pairs={{0,6},{1,13},{2,4},{3,15},{4,2},{5,9},{6,0},{7,11},{8,14},{9,5},{1... | collective-permute-start | bytes 196616 | tf_op jit(solution)/shard_map/ppermute | solution.py:360
  28.0 1.4 %shard_map.56._ = bf16[1024,1024]{1,0:T(8,128)(2,1)S(1)} custom-call(), custom_call_target="tpu_custom_call" | custom-call | flops 16777216 | bytes 1048576 | tf_op jit(solution)/shard_map/pallas_call | solution.py:47
  29.4 0.0 collective-permute-done.1.refs_1_
  29.4 0.8 %collective-permute-start.5 = (bf16[128,256]{1,0:T(8,128)(2,1)S(1)}, bf16[128,256]{1,0:T(8,128)(2,1)S(1)}, u32[]{:S(2)}, u32[]{:S(2)}) collective-permute-start(bf16[128,256]{1,0:T(8,128)(2,1)S(1)} %get-tuple-element.22), channel_id=1, source_target_pairs={{0,12},{1,11},{2,14},{3,9},{4,8},{5,15},{6,10},{7,13},{8,4},{9,3},... | collective-permute-start | bytes 196616 | tf_op jit(solution)/shard_map/ppermute | solution.py:360
  30.2 0.1 collective-permute-done.2.refs_2_
  30.3 1.7 %collective-permute-start.6 = (bf16[128,256]{1,0:T(8,128)(2,1)S(1)}, bf16[128,256]{1,0:T(8,128)(2,1)S(1)}, u32[]{:S(2)}, u32[]{:S(2)}) collective-permute-start(bf16[128,256]{1,0:T(8,128)(2,1)S(1)} %get-tuple-element.23), channel_id=1, source_target_pairs={{0,8},{1,3},{2,10},{3,1},{4,12},{5,7},{6,14},{7,5},{8,0},{9,11},{1... | collective-permute-start | bytes 196616 | tf_op jit(solution)/shard_map/ppermute | solution.py:360
  32.0 0.0 collective-permute-done.other_ref
  32.0 0.9 %collective-permute-start.7 = (bf16[128,256]{1,0:T(8,128)(2,1)S(1)}, bf16[128,256]{1,0:T(8,128)(2,1)S(1)}, u32[]{:S(2)}, u32[]{:S(2)}) collective-permute-start(bf16[128,256]{1,0:T(8,128)(2,1)S(1)} %get-tuple-element.24), channel_id=1, source_target_pairs={{0,4},{1,9},{2,6},{3,11},{4,0},{5,13},{6,2},{7,15},{8,12},{9,1},{1... | collective-permute-start | bytes 196616 | tf_op jit(solution)/shard_map/ppermute | solution.py:360
  33.0 2.6 %shard_map.57.waves_ref = bf16[1024,1024]{1,0:T(8,128)(2,1)S(1)} custom-call(bf16[8,64,384]{2,1,0:T(8,128)(2,1)S(1)} %all_to_all.10.own_ref, bf16[8,64,384]{2,1,0:T(8,128)(2,1)S(1)} %collective-permute-done.other_ref, bf16[1024,1024]{1,0:T(8,128)(2,1)S(1)} %shard_map.56._), custom_call_target="tpu_custom_call", output_to_operand_aliasing={{}: (2, {})} | custom-call | flops 2147483648 | bytes 1048576 | tf_op jit(solution)/shard_map/pallas_call | solution.py:47
  35.6 0.0 collective-permute-done.3.refs_3_
  35.6 0.0 collective-permute-done.4.refs_4_
  35.6 0.0 collective-permute-done.5.refs_5_
  35.7 0.0 collective-permute-done.6.refs_6_
  35.7 0.6 %collective-permute-done.7.refs_7_ = bf16[128,256]{1,0:T(8,128)(2,1)S(1)} collective-permute-done((bf16[128,256]{1,0:T(8,128)(2,1)S(1)}, bf16[128,256]{1,0:T(8,128)(2,1)S(1)}, u32[]{:S(2)}, u32[]{:S(2)}) %collective-permute-start.7) | collective-permute-done | bytes 65568 | tf_op jit(solution)/shard_map/ppermute | solution.py:360
  36.3 3.8 %shard_map.58 = (bf16[16,2,16,128]{3,2,1,0:T(8,128)(2,1)S(1)}, bf16[16,2,16,128]{3,2,1,0:T(8,128)(2,1)S(1)}) custom-call(bf16[8,64,384]{2,1,0:T(8,128)(2,1)S(1)} %all_to_all.10.own_ref, bf16[8,64,384]{2,1,0:T(8,128)(2,1)S(1)} %collective-permute-done.other_ref, bf16[1024,1024]{1,0:T(8,128)(2,1)S(1)} %shard_map.57.waves_ref, ...), custom_call_target="tpu_custom_call" | custom-call | flops 4831838208 | bytes 1048576 | tf_op jit(solution)/shard_map/pallas_call | solution.py:47
  40.1 0.1 collective-permute-start.8
  40.2 1.3 %collective-permute-done.8.other_ref = bf16[16,2,16,128]{3,2,1,0:T(8,128)(2,1)S(1)} collective-permute-done((bf16[16,2,16,128]{3,2,1,0:T(8,128)(2,1)S(1)}, bf16[16,2,16,128]{3,2,1,0:T(8,128)(2,1)S(1)}, u32[]{:S(2)}, u32[]{:S(2)}) %collective-permute-start.8) | collective-permute-done | bytes 131104 | tf_op jit(solution)/shard_map/ppermute | solution.py:405
  41.6 11.6 %all_to_all.11 = bf16[16,2,16,128]{3,2,1,0:T(8,128)(2,1)S(1)} all-to-all(bf16[16,2,16,128]{3,2,1,0:T(8,128)(2,1)S(1)} %shard_map.59), channel_id=1, replica_groups=mesh['ph'=2,'pl'=4,'bx'=2,'bc'=2] {'ph','pl','bx'}, dimensions={0} | all-to-all | bytes 262144 | tf_op jit(solution)/shard_map/all_to_all | solution.py:410
  53.2 1.4 %shard_map.60 = f32[23,16,128]{2,1,0:T(8,128)} custom-call(s32[2,8]{1,0:T(2,128)} %bitcast.11, bf16[2,4,2,2,16,128]{5,4,3,2,1,0:T(8,128)(2,1)S(1)} %bitcast.6), custom_call_target="tpu_custom_call" | custom-call | bytes 1048576 | tf_op jit(solution)/shard_map/pallas_call | solution.py:47
  (1 shorter events, 0.0 us)
Async XLA Ops:
  22.2 9.9 %collective-permute-start = (bf16[8,64,384]{2,1,0:T(8,128)(2,1)S(1)}, bf16[8,64,384]{2,1,0:T(8,128)(2,1)S(1)}, u32[]{:S(2)}, u32[]{:S(2)}) collective-permute-start(bf16[8,64,384]{2,1,0:T(8,128)(2,1)S(1)} %all_to_all.10.own_ref), channel_id=1, source_target_pairs={{0,1},{1,0},{2,3},{3,2},{4,5},{5,4},{6,7},{7,6},{8,9},{9,8},{10,11... | collective-permute-start | bytes 1179656 | tf_op jit(solution)/shard_map/ppermute | solution.py:363
  22.2 7.2 %collective-permute-start.1 = (bf16[128,256]{1,0:T(8,128)(2,1)S(1)}, bf16[128,256]{1,0:T(8,128)(2,1)S(1)}, u32[]{:S(2)}, u32[]{:S(2)}) collective-permute-start(bf16[128,256]{1,0:T(8,128)(2,1)S(1)} %get-tuple-element.18), channel_id=1, source_target_pairs={{0,2},{1,5},{2,0},{3,7},{4,6},{5,1},{6,4},{7,3},{8,10},{9,13},{10,... | collective-permute-start | bytes 196616 | tf_op jit(solution)/shard_map/ppermute | solution.py:360
  23.7 6.6 %collective-permute-start.2 = (bf16[128,256]{1,0:T(8,128)(2,1)S(1)}, bf16[128,256]{1,0:T(8,128)(2,1)S(1)}, u32[]{:S(2)}, u32[]{:S(2)}) collective-permute-start(bf16[128,256]{1,0:T(8,128)(2,1)S(1)} %get-tuple-element.19), channel_id=1, source_target_pairs={{0,14},{1,15},{2,12},{3,13},{4,10},{5,11},{6,8},{7,9},{8,6},{9,7},... | collective-permute-start | bytes 196616 | tf_op jit(solution)/shard_map/ppermute | solution.py:360
  24.4 11.3 %collective-permute-start.3 = (bf16[128,256]{1,0:T(8,128)(2,1)S(1)}, bf16[128,256]{1,0:T(8,128)(2,1)S(1)}, u32[]{:S(2)}, u32[]{:S(2)}) collective-permute-start(bf16[128,256]{1,0:T(8,128)(2,1)S(1)} %get-tuple-element.20), channel_id=1, source_target_pairs={{0,10},{1,7},{2,8},{3,5},{4,14},{5,3},{6,12},{7,1},{8,2},{9,15},{1... | collective-permute-start | bytes 196616 | tf_op jit(solution)/shard_map/ppermute | solution.py:360
  27.1 8.5 %collective-permute-start.4 = (bf16[128,256]{1,0:T(8,128)(2,1)S(1)}, bf16[128,256]{1,0:T(8,128)(2,1)S(1)}, u32[]{:S(2)}, u32[]{:S(2)}) collective-permute-start(bf16[128,256]{1,0:T(8,128)(2,1)S(1)} %get-tuple-element.21), channel_id=1, source_target_pairs={{0,6},{1,13},{2,4},{3,15},{4,2},{5,9},{6,0},{7,11},{8,14},{9,5},{1... | collective-permute-start | bytes 196616 | tf_op jit(solution)/shard_map/ppermute | solution.py:360
  29.4 6.2 %collective-permute-start.5 = (bf16[128,256]{1,0:T(8,128)(2,1)S(1)}, bf16[128,256]{1,0:T(8,128)(2,1)S(1)}, u32[]{:S(2)}, u32[]{:S(2)}) collective-permute-start(bf16[128,256]{1,0:T(8,128)(2,1)S(1)} %get-tuple-element.22), channel_id=1, source_target_pairs={{0,12},{1,11},{2,14},{3,9},{4,8},{5,15},{6,10},{7,13},{8,4},{9,3},... | collective-permute-start | bytes 196616 | tf_op jit(solution)/shard_map/ppermute | solution.py:360
  30.3 5.4 %collective-permute-start.6 = (bf16[128,256]{1,0:T(8,128)(2,1)S(1)}, bf16[128,256]{1,0:T(8,128)(2,1)S(1)}, u32[]{:S(2)}, u32[]{:S(2)}) collective-permute-start(bf16[128,256]{1,0:T(8,128)(2,1)S(1)} %get-tuple-element.23), channel_id=1, source_target_pairs={{0,8},{1,3},{2,10},{3,1},{4,12},{5,7},{6,14},{7,5},{8,0},{9,11},{1... | collective-permute-start | bytes 196616 | tf_op jit(solution)/shard_map/ppermute | solution.py:360
  32.0 4.3 %collective-permute-start.7 = (bf16[128,256]{1,0:T(8,128)(2,1)S(1)}, bf16[128,256]{1,0:T(8,128)(2,1)S(1)}, u32[]{:S(2)}, u32[]{:S(2)}) collective-permute-start(bf16[128,256]{1,0:T(8,128)(2,1)S(1)} %get-tuple-element.24), channel_id=1, source_target_pairs={{0,4},{1,9},{2,6},{3,11},{4,0},{5,13},{6,2},{7,15},{8,12},{9,1},{1... | collective-permute-start | bytes 196616 | tf_op jit(solution)/shard_map/ppermute | solution.py:360
  40.1 1.4 %collective-permute-start.8 = (bf16[16,2,16,128]{3,2,1,0:T(8,128)(2,1)S(1)}, bf16[16,2,16,128]{3,2,1,0:T(8,128)(2,1)S(1)}, u32[]{:S(2)}, u32[]{:S(2)}) collective-permute-start(bf16[16,2,16,128]{3,2,1,0:T(8,128)(2,1)S(1)} %get-tuple-element.26), channel_id=1, source_target_pairs={{0,1},{1,0},{2,3},{3,2},{4,5},{5,4},{6,7},{7,6},{8,9},{9,8},{10,11... | collective-permute-start | bytes 393224 | tf_op jit(solution)/shard_map/ppermute | solution.py:405
where the time goes:
time: 54.9 us; the launch traced here: 54.6 us
  blocking collectives  31 us (56%)
  Pallas kernels  12.1 us (22%)
  starting transfers between devices  9.41 us (17%)
  waiting for transfers between devices  2.06 us (4%)
    all_to_all x1, blocking collectives, on_device(): lax.all_to_all(send, pair_axes, split_axis=0, concat_axis=0, tiled=True)  19.4 us
    pallas_call x6, Pallas kernels, call(): pl.pallas_call(body, out_shape=shapes, in_specs=specs, out_specs=out_spec...  12.1 us
    all_to_all x1, blocking collectives, on_device(): lax.all_to_all(partial, ('ph', 'pl', 'bx'), split_axis=0, concat_axis=0,...  11.6 us
    ppermute x7, starting transfers between devices, on_device(): screens.append(lax.ppermute(screen_sends[step], ('pl', 'bx', 'bc'), to))  9.33 us
    ppermute x1, waiting for transfers between devices, on_device(): taken = lax.ppermute(give, 'bc', [(i, i ^ 1) for i in range(groups)])  1.33 us
  transfers between devices with their start and end apart: 9, of which 3 were waited for; matrix products, arithmetic and copies ran while one was open for 0% of the time, Pallas kernels for 7%

commit v1 on v0

--- a/solution.py
+++ b/solution.py
@@ -1,3 +1,4 @@
+import functools
 import math
 
 import jax
@@ -29,14 +30,14 @@
     return lax.dot_general(a, b, (((1,), (1,)), ((), ())), preferred_element_type=F32)
 
 
-SPACES = {"s": pltpu.SMEM, "v": pltpu.VMEM, "h": pl.ANY}
+SPACES = {"s": pltpu.SMEM, "m": pltpu.SMEM, "v": pltpu.VMEM, "h": pl.ANY}
 
 
 def call(body, inputs, outputs, scratch=(), flops=0, aliases=None):
     specs, arrays = [], []
     for space, array in inputs:
         specs.append(pl.BlockSpec(memory_space=SPACES.get(space, pltpu.VMEM)))
-        home = pltpu.VMEM if space == "v" else pltpu.HBM
+        home = {"v": pltpu.VMEM, "m": pltpu.SMEM}.get(space, pltpu.HBM)
         array = pltpu.with_memory_space_constraint(array, home)
         arrays.append(array)
     shapes, out_specs = [], []
@@ -57,7 +58,8 @@
 
 
 def pack_kernel(kpts_ref, q_ref, orbital_ref, trial_ref, screen_ref, out_ref, *refs):
-    *sends, room, table, ordered, fetch_sems, send_sems, table_sem = refs
+    *sends, basis_ref, room, table, ordered, cos_low, sin_low, cos_high, sin_high = refs[:-3]
+    fetch_sems, send_sems, table_sem = refs[-3:]
     bx, bc = lax.axis_index("bx"), lax.axis_index("bc")
     strips, low = lax.axis_size("bx"), room.shape[0]
     points = orbital_ref.shape[2]
@@ -76,6 +78,8 @@
             fetch.start()
     table_fetch = pltpu.make_async_copy(screen_ref, table, table_sem)
     table_fetch.start()
+    basis_tables(cos_low, sin_low, cos_high, sin_high)
+    basis_rows(basis_ref, cos_low, sin_low, cos_high, sin_high)
     copies = []
     for d in range(low):
         for fetch in fetches[d]:
@@ -105,8 +109,13 @@
         copy.wait()
 
 
-def basis_kernel(rows, cos_low, sin_low, cos_high, sin_high):
-    columns = rows.shape[1]
+def basis_kernel(basis_ref, *tables):
+    basis_tables(*tables)
+    basis_rows(basis_ref, *tables)
+
+
+def basis_tables(cos_low, sin_low, cos_high, sin_high):
+    columns = cos_low.shape[1]
     quarter = columns // 4
     groups = lax.axis_size("bc")
     strip = NG // (lax.axis_size("bx") * groups)
@@ -140,13 +149,19 @@
     table(2, 1, cos_low, sin_low, math.sqrt(2.0 / NR))
     table(2 * TABLE, 0, cos_high, sin_high, 1.0)
 
+
+def basis_rows(basis_ref, cos_low, sin_low, cos_high, sin_high):
+    half = basis_ref.shape[2]
+
     def step(block, carry):
         high = pl.ds(block, 1)
-        value = cos_low[...] * cos_high[high, :] - sin_low[...] * sin_high[high, :]
-        rows[pl.ds(pl.multiple_of(block * TABLE, TABLE), TABLE), :] = value.astype(BF16)
+        value = (cos_low[...] * cos_high[high, :] - sin_low[...] * sin_high[high, :]).astype(BF16)
+        rows = pl.ds(pl.multiple_of(block * TABLE, TABLE), TABLE)
+        for kind in range(2):
+            basis_ref[kind, rows, :] = value[:, kind * half : (kind + 1) * half]
         return carry
 
-    lax.fori_loop(0, rows.shape[0] // TABLE, step, 0)
+    lax.fori_loop(0, basis_ref.shape[1] // TABLE, step, 0)
 
 
 def distances(count):
@@ -159,37 +174,34 @@
     return jnp.where(lax.axis_index("bc") % 2 == 0, pair[0], pair[1])
 
 
-def waves_kernel(own_ref, other_ref, _, waves_ref, first, second, even, odd):
+def waves_kernel(own, orbital_ref, _, waves_ref, sets, even, odd):
     side = lax.axis_index("bc")
-    blocks, _, _ = own_ref.shape
+    kind = side if own else 1 - side
+    blocks, _, _ = orbital_ref.shape
     points = NR // blocks
     piece = 256 if points % 256 == 0 else LANES
     middle = NR // 2
-    quarter = waves_ref.shape[1] // 4
+    quarter = waves_ref.shape[2] // 2
     source = lax.broadcasted_iota(jnp.int32, (piece, piece), 0)
     target = lax.broadcasted_iota(jnp.int32, (piece, piece), 1)
     flip = jnp.where(source + target == piece - 1, 1.0, 0.0).astype(BF16)
-    for slot, ref in ((side, own_ref), (1 - side, other_ref)):
-        for start in range(0, middle, piece):
-            ahead = ref[start // points, :, start % points : start % points + piece].astype(F32)
-            mirror = NR - start - piece
-            behind = dot(ref[mirror // points, :, mirror % points : mirror % points + piece], flip)
-            for half_of, value in enumerate((ahead, behind)):
-                first[slot, half_of, :, start : start + piece] = value[:NV]
-                second[slot, half_of, :, start : start + piece] = value[NV:]
-
-    for kind in (1, 0):
-        outer, inner = (second, first) if kind else (first, second)
-        for v in range(NV):
-            rows = slice(v * NV, (v + 1) * NV)
-            ahead = outer[kind, 0, v : v + 1, :] * inner[kind, 0]
-            behind = outer[kind, 1, v : v + 1, :] * inner[kind, 1]
-            even[kind, rows, :] = (ahead + behind).astype(BF16)
-            odd[kind, rows, :] = (ahead - behind).astype(BF16)
-        spans = [slice((2 * kind + parity) * quarter, (2 * kind + parity + 1) * quarter) for parity in range(2)]
-        results = [dot(x[kind], waves_ref[:, span]).astype(BF16) for x, span in zip((even, odd), spans)]
-        for span, result in zip(spans, results):
-            waves_ref[:, span] = result
+    for start in range(0, middle, piece):
+        ahead = orbital_ref[start // points, :, start % points : start % points + piece].astype(F32)
+        mirror = NR - start - piece
+        behind = dot(orbital_ref[mirror // points, :, mirror % points : mirror % points + piece], flip)
+        for half_of, value in enumerate((ahead, behind)):
+            sets[kind, half_of, :, start : start + piece] = value[:NV]
+            sets[1 - kind, half_of, :, start : start + piece] = value[NV:]
+    for v in range(NV):
+        rows = slice(v * NV, (v + 1) * NV)
+        ahead = sets[0, 0, v : v + 1, :] * sets[1, 0]
+        behind = sets[0, 1, v : v + 1, :] * sets[1, 1]
+        even[rows, :] = (ahead + behind).astype(BF16)
+        odd[rows, :] = (ahead - behind).astype(BF16)
+    spans = (slice(0, quarter), slice(quarter, 2 * quarter))
+    results = [dot(x[...], waves_ref[kind, :, span]).astype(BF16) for x, span in zip((even, odd), spans)]
+    for span, result in zip(spans, results):
+        waves_ref[kind, :, span] = result
 
 
 def pair_kernel(own_ref, other_ref, waves_ref, *refs):
@@ -205,8 +217,8 @@
     broad = screen.shape[2]
     for parity in range(2):
         for s in range(strips):
-            source, target = half + parity * quarter + s * run, (2 * s + parity) * run
-            conduction[:, target : target + run] = waves_ref[:, source : source + run]
+            source, target = parity * quarter + s * run, (2 * s + parity) * run
+            conduction[:, target : target + run] = waves_ref[1, :, source : source + run]
     if len(screens) > 1:
         me = lax.axis_index(("pl", "bx"))
         part = screens[0].shape[0] // 2
@@ -235,7 +247,7 @@
                 diagonal[kind, j * LANES + r * NV : j * LANES + (r + 1) * NV, :] = rows * masks[r]
 
     for s in range(strips):
-        screened[:, s * broad : (s + 1) * broad] = dot(waves_ref[:, :half], screen[s]).astype(BF16)
+        screened[:, s * broad : (s + 1) * broad] = dot(waves_ref[0], screen[s]).astype(BF16)
 
     groups = NVC // LANES
     scale = 1.0 / math.sqrt(NVC) / math.sqrt(NG)
@@ -312,9 +324,11 @@
     aligned = points % LANES == 0 and states % LANES == 0 and pair_count & (pair_count - 1) == 0
     orbital_t, trial_t = orbitals.transpose(1, 2, 0), trial.transpose(1, 2, 0)
     kpts_t = pair_kpts.T
+    basis_out = [("v", (2, NR // 2, half), BF16)]
+    tables = [pltpu.VMEM((TABLE, 2 * half), F32)] * 4
 
     if aligned:
-        send, *screen_sends = call(
+        send, *screen_sends, basis = call(
             pack_kernel,
             [
                 ("s", kpts_t),
@@ -323,11 +337,12 @@
                 ("h", trial_t),
                 ("h", screening.reshape(tall * kinds, broad)),
             ],
-            [("h", (pair_count, count, points + states), BF16)] + [("b", (tall, broad), BF16)] * (low * strips),
+            [("h", (pair_count, count, points + states), BF16)] + [("b", (tall, broad), BF16)] * (low * strips) + basis_out,
             [
                 pltpu.VMEM((low, count, points + states), BF16),
                 pltpu.VMEM((tall * kinds, broad), BF16),
                 pltpu.VMEM((broad // LANES, tall * kinds, LANES), F32),
+                *tables,
                 pltpu.SemaphoreType.DMA((low, 3)),
                 pltpu.SemaphoreType.DMA((halves, low)),
                 pltpu.SemaphoreType.DMA,
@@ -342,15 +357,9 @@
         trial_part = trial_t[lax.dynamic_index_in_dim(near, bc, 1, keepdims=False)]
         send = jnp.concatenate([orbital_part, trial_part], axis=2)
         send = jnp.concatenate([send] * halves, axis=0)
+        basis = call(basis_kernel, [], basis_out, tables, flops=NR * NG)[0]
         screen_send = screening.transpose(1, 0, 2)[pair_q]
     got = lax.all_to_all(send, pair_axes, split_axis=0, concat_axis=0, tiled=True)
-    basis = call(
-        basis_kernel,
-        [],
-        [("v", (NR // 2, 2 * half), BF16)],
-        [pltpu.VMEM((TABLE, 2 * half), F32)] * 4,
-        flops=NR * NG * 8,
-    )[0]
     if aligned:
         screens = list(screen_sends[:1])
         for step, distance in list(enumerate(distances(low * strips)))[1:]:
@@ -378,14 +387,16 @@
     lanes = LANES // NV * count
     places = states if aligned else NVC
     shape = (NVC // places * strips, 2, share, places)
-    waves = call(
-        waves_kernel,
-        [("v", got), ("v", other), ("v", basis)],
-        [("v", (NR // 2, 2 * half), BF16)],
-        [pltpu.VMEM((2, 2, NV, NR // 2), F32)] * 2 + [pltpu.VMEM((2, NVC, NR // 2), BF16)] * 2,
-        flops=2 * NVC * NR * half,
-        aliases={2: 0},
-    )[0]
+    waves = basis
+    for own, half_of_bands in ((True, got), (False, other)):
+        waves = call(
+            functools.partial(waves_kernel, own),
+            [("v", half_of_bands), ("v", waves)],
+            basis_out,
+            [pltpu.VMEM((2, 2, NV, NR // 2), F32)] + [pltpu.VMEM((NVC, NR // 2), BF16)] * 2,
+            flops=NVC * NR * half,
+            aliases={1: 0},
+        )[0]
     keep, give = call(
         pair_kernel,
         [("v", got), ("v", other), ("v", waves)] + [("v", x) for x in screens],
@@ -410,7 +421,7 @@
     out_got = lax.all_to_all(partial, ("ph", "pl", "bx"), split_axis=0, concat_axis=0, tiled=True)
     out_got = out_got.reshape(halves, low, strips, 2, share, states)
     if aligned:
-        applied = call(gather_kernel, [("s", kpts_t), ("v", out_got)], [("b", (kpt_count, share, states), F32)])[0]
+        applied = call(gather_kernel, [("m", kpts_t), ("v", out_got)], [("b", (kpt_count, share, states), F32)])[0]
     else:
         summed = jnp.sum(out_got.astype(F32), axis=0).reshape(-1, share * states)
         hot = (pair_kpts.reshape(-1)[None, :] == jnp.arange(kpt_count)[:, None]).astype(F32)

time: 54.9 us -> 55.1 us (level)
  waiting for transfers between devices: 2.06 us -> 3.19 us
  Pallas kernels: 12.1 us -> 11.1 us
    ppermute x7, waiting for transfers between devices: 0.72 us -> 1.85 us  [on_device(): screens.append(lax.ppermute(screen_sends[step], ('pl', 'bx', 'bc'), to))]
    pallas_call x6, Pallas kernels: 12.1 us -> 11.1 us  [call(): pl.pallas_call(body, out_shape=shapes, in_specs=specs, out_specs=out_spec...]
  transfers between devices with their start and end apart: 9 -> 9, of which waited for: 3 -> 4; matrix products, arithmetic and copies ran while one was open for 0% -> 0% of each run, Pallas kernels for 7% -> 5%
where the time goes in v1:
time: 55.1 us; the launch traced here: 54.8 us
  blocking collectives  31 us (56%)
  Pallas kernels  11.1 us (20%)
  starting transfers between devices  9.48 us (17%)
  waiting for transfers between devices  3.19 us (6%)
    all_to_all x1, blocking collectives, on_device(): lax.all_to_all(send, pair_axes, split_axis=0, concat_axis=0, tiled=True)  19.4 us
    all_to_all x1, blocking collectives, on_device(): lax.all_to_all(partial, ('ph', 'pl', 'bx'), split_axis=0, concat_axis=0,...  11.6 us
    pallas_call x6, Pallas kernels, call(): pl.pallas_call(body, out_shape=shapes, in_specs=specs, out_specs=out_spec...  11.1 us
    ppermute x7, starting transfers between devices, on_device(): screens.append(lax.ppermute(screen_sends[step], ('pl', 'bx', 'bc'), to))  9.4 us
    ppermute x7, waiting for transfers between devices, on_device(): screens.append(lax.ppermute(screen_sends[step], ('pl', 'bx', 'bc'), to))  1.85 us
    ppermute x1, waiting for transfers between devices, on_device(): taken = lax.ppermute(give, 'bc', [(i, i ^ 1) for i in range(groups)])  1.33 us
  transfers between devices with their start and end apart: 9, of which 4 were waited for; matrix products, arithmetic and copies ran while one was open for 0% of the time, Pallas kernels for 5%

profile of v1, /device:TPU:0, one launch (start us, length us, event | category | flops | bytes accessed | tf_op | source)
XLA Modules:
  0.0 54.8 jit_solution(8014221907266115358)
XLA Ops:
  0.0 3.0 %shard_map.55 = (bf16[8,64,384]{2,1,0:T(8,128)(2,1)}, bf16[128,256]{1,0:T(8,128)(2,1)S(1)}, bf16[128,256]{1,0:T(8,128)(2,1)S(1)}, bf16[128,256]{1,0:T(8,128)(2,1...) custom-call(s32[2,8]{1,0:T(2,128)} %bitcast.7, ...), custom_call_target="tpu_custom_call" | custom-call | flops 268435456 | bytes 1048576 | tf_op jit(solution)/shard_map/pallas_call | solution.py:48
  3.1 19.4 %all_to_all.10.orbital_ref.own_ref = bf16[8,64,384]{2,1,0:T(8,128)(2,1)S(1)} all-to-all(bf16[8,64,384]{2,1,0:T(8,128)(2,1)} %get-tuple-element.17), channel_id=1, replica_groups=mesh['ph'=2,'pl'=4,'bx'=2,'bc'=2] {'ph','pl'}, dimensions={0} | all-to-all | bytes 786432 | tf_op jit(solution)/shard_map/all_to_all | solution.py:362
  22.4 0.0 collective-permute-start
  22.4 1.5 %collective-permute-start.1 = (bf16[128,256]{1,0:T(8,128)(2,1)S(1)}, bf16[128,256]{1,0:T(8,128)(2,1)S(1)}, u32[]{:S(2)}, u32[]{:S(2)}) collective-permute-start(bf16[128,256]{1,0:T(8,128)(2,1)S(1)} %get-tuple-element.20), channel_id=1, source_target_pairs={{0,2},{1,5},{2,0},{3,7},{4,6},{5,1},{6,4},{7,3},{8,10},{9,13},{10,... | collective-permute-start | bytes 196616 | tf_op jit(solution)/shard_map/ppermute | solution.py:369
  23.9 0.7 %collective-permute-start.2 = (bf16[128,256]{1,0:T(8,128)(2,1)S(1)}, bf16[128,256]{1,0:T(8,128)(2,1)S(1)}, u32[]{:S(2)}, u32[]{:S(2)}) collective-permute-start(bf16[128,256]{1,0:T(8,128)(2,1)S(1)} %get-tuple-element.21), channel_id=1, source_target_pairs={{0,14},{1,15},{2,12},{3,13},{4,10},{5,11},{6,8},{7,9},{8,6},{9,7},... | collective-permute-start | bytes 196616 | tf_op jit(solution)/shard_map/ppermute | solution.py:369
  24.6 2.7 %collective-permute-start.3 = (bf16[128,256]{1,0:T(8,128)(2,1)S(1)}, bf16[128,256]{1,0:T(8,128)(2,1)S(1)}, u32[]{:S(2)}, u32[]{:S(2)}) collective-permute-start(bf16[128,256]{1,0:T(8,128)(2,1)S(1)} %get-tuple-element.22), channel_id=1, source_target_pairs={{0,10},{1,7},{2,8},{3,5},{4,14},{5,3},{6,12},{7,1},{8,2},{9,15},{1... | collective-permute-start | bytes 196616 | tf_op jit(solution)/shard_map/ppermute | solution.py:369
  27.4 0.9 %collective-permute-start.4 = (bf16[128,256]{1,0:T(8,128)(2,1)S(1)}, bf16[128,256]{1,0:T(8,128)(2,1)S(1)}, u32[]{:S(2)}, u32[]{:S(2)}) collective-permute-start(bf16[128,256]{1,0:T(8,128)(2,1)S(1)} %get-tuple-element.23), channel_id=1, source_target_pairs={{0,6},{1,13},{2,4},{3,15},{4,2},{5,9},{6,0},{7,11},{8,14},{9,5},{1... | collective-permute-start | bytes 196616 | tf_op jit(solution)/shard_map/ppermute | solution.py:369
  28.3 1.5 %shard_map.56._ = bf16[2,1024,512]{2,1,0:T(8,128)(2,1)S(1)} custom-call(bf16[8,64,384]{2,1,0:T(8,128)(2,1)S(1)} %all_to_all.10.orbital_ref.own_ref, bf16[2,1024,512]{2,1,0:T(8,128)(2,1)S(1)} %get-tuple-element.18._), custom_call_target="tpu_custom_call", output_to_operand_aliasing={{}: (1, {})} | custom-call | flops 1073741824 | bytes 1048576 | tf_op jit(solution)/shard_map/pallas_call | solution.py:48
  29.7 0.0 collective-permute-done.1.refs_1_
  29.8 0.8 %collective-permute-start.5 = (bf16[128,256]{1,0:T(8,128)(2,1)S(1)}, bf16[128,256]{1,0:T(8,128)(2,1)S(1)}, u32[]{:S(2)}, u32[]{:S(2)}) collective-permute-start(bf16[128,256]{1,0:T(8,128)(2,1)S(1)} %get-tuple-element.24), channel_id=1, source_target_pairs={{0,12},{1,11},{2,14},{3,9},{4,8},{5,15},{6,10},{7,13},{8,4},{9,3},... | collective-permute-start | bytes 196616 | tf_op jit(solution)/shard_map/ppermute | solution.py:369
  30.6 0.0 collective-permute-done.2.refs_2_
  30.6 1.8 %collective-permute-start.6 = (bf16[128,256]{1,0:T(8,128)(2,1)S(1)}, bf16[128,256]{1,0:T(8,128)(2,1)S(1)}, u32[]{:S(2)}, u32[]{:S(2)}) collective-permute-start(bf16[128,256]{1,0:T(8,128)(2,1)S(1)} %get-tuple-element.25), channel_id=1, source_target_pairs={{0,8},{1,3},{2,10},{3,1},{4,12},{5,7},{6,14},{7,5},{8,0},{9,11},{1... | collective-permute-start | bytes 196616 | tf_op jit(solution)/shard_map/ppermute | solution.py:369
  32.4 0.0 collective-permute-done.orbital_ref.other_ref
  32.4 0.9 %collective-permute-start.7 = (bf16[128,256]{1,0:T(8,128)(2,1)S(1)}, bf16[128,256]{1,0:T(8,128)(2,1)S(1)}, u32[]{:S(2)}, u32[]{:S(2)}) collective-permute-start(bf16[128,256]{1,0:T(8,128)(2,1)S(1)} %get-tuple-element.26), channel_id=1, source_target_pairs={{0,4},{1,9},{2,6},{3,11},{4,0},{5,13},{6,2},{7,15},{8,12},{9,1},{1... | collective-permute-start | bytes 196616 | tf_op jit(solution)/shard_map/ppermute | solution.py:369
  33.3 1.5 %shard_map.57.waves_ref = bf16[2,1024,512]{2,1,0:T(8,128)(2,1)S(1)} custom-call(bf16[8,64,384]{2,1,0:T(8,128)(2,1)S(1)} %collective-permute-done.orbital_ref.other_ref, bf16[2,1024,512]{2,1,0:T(8,128)(2,1)S(1)} %shard_map.56._), custom_call_target="tpu_custom_call", output_to_operand_aliasing={{}: (1, {})} | custom-call | flops 1073741824 | bytes 1048576 | tf_op jit(solution)/shard_map/pallas_call | solution.py:48
  34.8 0.0 collective-permute-done.3.refs_3_
  34.8 0.0 collective-permute-done.4.refs_4_
  34.8 0.6 %collective-permute-done.5.refs_5_ = bf16[128,256]{1,0:T(8,128)(2,1)S(1)} collective-permute-done((bf16[128,256]{1,0:T(8,128)(2,1)S(1)}, bf16[128,256]{1,0:T(8,128)(2,1)S(1)}, u32[]{:S(2)}, u32[]{:S(2)}) %collective-permute-start.5) | collective-permute-done | bytes 65568 | tf_op jit(solution)/shard_map/ppermute | solution.py:369
  35.4 0.4 collective-permute-done.6.refs_6_
  35.7 0.9 %collective-permute-done.7.refs_7_ = bf16[128,256]{1,0:T(8,128)(2,1)S(1)} collective-permute-done((bf16[128,256]{1,0:T(8,128)(2,1)S(1)}, bf16[128,256]{1,0:T(8,128)(2,1)S(1)}, u32[]{:S(2)}, u32[]{:S(2)}) %collective-permute-start.7) | collective-permute-done | bytes 65568 | tf_op jit(solution)/shard_map/ppermute | solution.py:369
  36.6 0.0 copy-start
  36.7 3.8 %shard_map.58 = (bf16[16,2,16,128]{3,2,1,0:T(8,128)(2,1)S(1)}, bf16[16,2,16,128]{3,2,1,0:T(8,128)(2,1)S(1)}) custom-call(bf16[8,64,384]{2,1,0:T(8,128)(2,1)S(1)} %all_to_all.10.orbital_ref.own_ref, bf16[8,64,384]{2,1,0:T(8,128)(2,1)S(1)} %collective-permute-done.orbital_ref.other_ref, bf16[2,1024,512]{2,1,0:T(8,128)(2,1)S(1)} %shard_map.57.waves_ref, ...), custom_call_target="tpu_custom_call" | custom-call | flops 4831838208 | bytes 1048576 | tf_op jit(solution)/shard_map/pallas_call | solution.py:48
  40.5 0.1 collective-permute-start.8
  40.6 1.3 %collective-permute-done.8.other_ref = bf16[16,2,16,128]{3,2,1,0:T(8,128)(2,1)S(1)} collective-permute-done((bf16[16,2,16,128]{3,2,1,0:T(8,128)(2,1)S(1)}, bf16[16,2,16,128]{3,2,1,0:T(8,128)(2,1)S(1)}, u32[]{:S(2)}, u32[]{:S(2)}) %collective-permute-start.8) | collective-permute-done | bytes 131104 | tf_op jit(solution)/shard_map/ppermute | solution.py:416
  41.9 11.6 %all_to_all.11 = bf16[16,2,16,128]{3,2,1,0:T(8,128)(2,1)S(1)} all-to-all(bf16[16,2,16,128]{3,2,1,0:T(8,128)(2,1)S(1)} %shard_map.59), channel_id=1, replica_groups=mesh['ph'=2,'pl'=4,'bx'=2,'bc'=2] {'ph','pl','bx'}, dimensions={0} | all-to-all | bytes 262144 | tf_op jit(solution)/shard_map/all_to_all | solution.py:421
  53.5 0.0 copy-done
  53.5 1.3 %shard_map.60 = f32[23,16,128]{2,1,0:T(8,128)} custom-call(s32[2,8]{1,0:T(2,128)S(1)} %bitcast.8, bf16[2,4,2,2,16,128]{5,4,3,2,1,0:T(8,128)(2,1)S(1)} %bitcast.6), custom_call_target="tpu_custom_call" | custom-call | bytes 1048576 | tf_op jit(solution)/shard_map/pallas_call | solution.py:48
  (1 shorter events, 0.0 us)
Async XLA Ops:
  22.4 10.0 %collective-permute-start = (bf16[8,64,384]{2,1,0:T(8,128)(2,1)S(1)}, bf16[8,64,384]{2,1,0:T(8,128)(2,1)S(1)}, u32[]{:S(2)}, u32[]{:S(2)}) collective-permute-start(bf16[8,64,384]{2,1,0:T(8,128)(2,1)S(1)} %all_to_all.10.orbital_ref.own_ref), channel_id=1, source_target_pairs={{0,1},{1,0},{2,3},{3,2},{4,5},{5,4},{6,7},{7,6},{8,9},{9,8},{10,11... | collective-permute-start | bytes 1179656 | tf_op jit(solution)/shard_map/ppermute | solution.py:372
  22.4 7.3 %collective-permute-start.1 = (bf16[128,256]{1,0:T(8,128)(2,1)S(1)}, bf16[128,256]{1,0:T(8,128)(2,1)S(1)}, u32[]{:S(2)}, u32[]{:S(2)}) collective-permute-start(bf16[128,256]{1,0:T(8,128)(2,1)S(1)} %get-tuple-element.20), channel_id=1, source_target_pairs={{0,2},{1,5},{2,0},{3,7},{4,6},{5,1},{6,4},{7,3},{8,10},{9,13},{10,... | collective-permute-start | bytes 196616 | tf_op jit(solution)/shard_map/ppermute | solution.py:369
  23.9 6.6 %collective-permute-start.2 = (bf16[128,256]{1,0:T(8,128)(2,1)S(1)}, bf16[128,256]{1,0:T(8,128)(2,1)S(1)}, u32[]{:S(2)}, u32[]{:S(2)}) collective-permute-start(bf16[128,256]{1,0:T(8,128)(2,1)S(1)} %get-tuple-element.21), channel_id=1, source_target_pairs={{0,14},{1,15},{2,12},{3,13},{4,10},{5,11},{6,8},{7,9},{8,6},{9,7},... | collective-permute-start | bytes 196616 | tf_op jit(solution)/shard_map/ppermute | solution.py:369
  24.6 10.2 %collective-permute-start.3 = (bf16[128,256]{1,0:T(8,128)(2,1)S(1)}, bf16[128,256]{1,0:T(8,128)(2,1)S(1)}, u32[]{:S(2)}, u32[]{:S(2)}) collective-permute-start(bf16[128,256]{1,0:T(8,128)(2,1)S(1)} %get-tuple-element.22), channel_id=1, source_target_pairs={{0,10},{1,7},{2,8},{3,5},{4,14},{5,3},{6,12},{7,1},{8,2},{9,15},{1... | collective-permute-start | bytes 196616 | tf_op jit(solution)/shard_map/ppermute | solution.py:369
  27.4 7.4 %collective-permute-start.4 = (bf16[128,256]{1,0:T(8,128)(2,1)S(1)}, bf16[128,256]{1,0:T(8,128)(2,1)S(1)}, u32[]{:S(2)}, u32[]{:S(2)}) collective-permute-start(bf16[128,256]{1,0:T(8,128)(2,1)S(1)} %get-tuple-element.23), channel_id=1, source_target_pairs={{0,6},{1,13},{2,4},{3,15},{4,2},{5,9},{6,0},{7,11},{8,14},{9,5},{1... | collective-permute-start | bytes 196616 | tf_op jit(solution)/shard_map/ppermute | solution.py:369
  29.8 5.6 %collective-permute-start.5 = (bf16[128,256]{1,0:T(8,128)(2,1)S(1)}, bf16[128,256]{1,0:T(8,128)(2,1)S(1)}, u32[]{:S(2)}, u32[]{:S(2)}) collective-permute-start(bf16[128,256]{1,0:T(8,128)(2,1)S(1)} %get-tuple-element.24), channel_id=1, source_target_pairs={{0,12},{1,11},{2,14},{3,9},{4,8},{5,15},{6,10},{7,13},{8,4},{9,3},... | collective-permute-start | bytes 196616 | tf_op jit(solution)/shard_map/ppermute | solution.py:369
  30.6 5.2 %collective-permute-start.6 = (bf16[128,256]{1,0:T(8,128)(2,1)S(1)}, bf16[128,256]{1,0:T(8,128)(2,1)S(1)}, u32[]{:S(2)}, u32[]{:S(2)}) collective-permute-start(bf16[128,256]{1,0:T(8,128)(2,1)S(1)} %get-tuple-element.25), channel_id=1, source_target_pairs={{0,8},{1,3},{2,10},{3,1},{4,12},{5,7},{6,14},{7,5},{8,0},{9,11},{1... | collective-permute-start | bytes 196616 | tf_op jit(solution)/shard_map/ppermute | solution.py:369
  32.4 4.3 %collective-permute-start.7 = (bf16[128,256]{1,0:T(8,128)(2,1)S(1)}, bf16[128,256]{1,0:T(8,128)(2,1)S(1)}, u32[]{:S(2)}, u32[]{:S(2)}) collective-permute-start(bf16[128,256]{1,0:T(8,128)(2,1)S(1)} %get-tuple-element.26), channel_id=1, source_target_pairs={{0,4},{1,9},{2,6},{3,11},{4,0},{5,13},{6,2},{7,15},{8,12},{9,1},{1... | collective-permute-start | bytes 196616 | tf_op jit(solution)/shard_map/ppermute | solution.py:369
  36.6 16.9 %copy-start = (s32[8,2]{0,1:T(2,128)S(1)}, s32[8,2]{0,1:T(2,128)}, u32[]{:S(2)}) copy-start(s32[8,2]{0,1:T(2,128)} %param.8) | copy-start | bytes 196
  40.5 1.4 %collective-permute-start.8 = (bf16[16,2,16,128]{3,2,1,0:T(8,128)(2,1)S(1)}, bf16[16,2,16,128]{3,2,1,0:T(8,128)(2,1)S(1)}, u32[]{:S(2)}, u32[]{:S(2)}) collective-permute-start(bf16[16,2,16,128]{3,2,1,0:T(8,128)(2,1)S(1)} %get-tuple-element.28), channel_id=1, source_target_pairs={{0,1},{1,0},{2,3},{3,2},{4,5},{5,4},{6,7},{7,6},{8,9},{9,8},{10,11... | collective-permute-start | bytes 393224 | tf_op jit(solution)/shard_map/ppermute | solution.py:416

commit v2 on v1

--- a/solution.py
+++ b/solution.py
@@ -161,11 +161,11 @@
             basis_ref[kind, rows, :] = value[:, kind * half : (kind + 1) * half]
         return carry
 
-    lax.fori_loop(0, basis_ref.shape[1] // TABLE, step, 0)
+    lax.fori_loop(0, basis_ref.shape[1] // TABLE, step, 0, unroll=True)
 
 
 def distances(count):
-    order = [0] + [d for d in (1, 7, 5, 3, 6, 4, 2) if d < count]
+    order = [0] + [d for d in (7, 5, 6, 4, 3, 1, 2) if d < count]
     order += [d for d in range(1, count) if d not in order]
     return [(d, (d << 1) % count | (d << 1) // count) for d in order]
 
@@ -296,10 +296,6 @@
                 put(1, at + f, woven[f * count : (f + 1) * count].astype(BF16))
     keep_ref[...] = shares[side]
     give_ref[...] = shares[1 - side]
-
-
-def add_kernel(one_ref, other_ref, out_ref):
-    out_ref[...] = (one_ref[...].astype(F32) + other_ref[...].astype(F32)).astype(BF16)
 
 
 def gather_kernel(kpts_ref, got_ref, out_ref):
@@ -414,7 +410,7 @@
         flops=2 * NVC * half * half + 8 * NVC * NVC * half,
     )
     taken = lax.ppermute(give, "bc", [(i, i ^ 1) for i in range(groups)])
-    partial = call(add_kernel, [("v", keep), ("v", taken)], [("v", shape, BF16)])[0]
+    partial = (keep.astype(F32) + taken.astype(F32)).astype(BF16)
     if not aligned:
         partial = partial.reshape(strips, 2, share, pair_count, states).transpose(3, 0, 1, 2, 4)
         partial = partial.reshape(pair_count * strips, 2, share, states)

time: 55.1 us -> 55 us (level)
    pallas_call x6 -> x5, Pallas kernels: 11.1 us -> 11 us  [call(): pl.pallas_call(body, out_shape=shapes, in_specs=specs, out_specs=out_spec...]
where the time goes in v2:
time: 55 us; the launch traced here: 54.8 us
  blocking collectives  31 us (56%)
  Pallas kernels  11 us (20%)
  starting transfers between devices  9.48 us (17%)
  waiting for transfers between devices  3.19 us (6%)
    all_to_all x1, blocking collectives, on_device(): lax.all_to_all(send, pair_axes, split_axis=0, concat_axis=0, tiled=True)  19.4 us
    all_to_all x1, blocking collectives, on_device(): lax.all_to_all(partial, ('ph', 'pl', 'bx'), split_axis=0, concat_axis=0,...  11.6 us
    pallas_call x5, Pallas kernels, call(): pl.pallas_call(body, out_shape=shapes, in_specs=specs, out_specs=out_spec...  11 us
    ppermute x7, starting transfers between devices, on_device(): screens.append(lax.ppermute(screen_sends[step], ('pl', 'bx', 'bc'), to))  9.4 us
    ppermute x7, waiting for transfers between devices, on_device(): screens.append(lax.ppermute(screen_sends[step], ('pl', 'bx', 'bc'), to))  1.85 us
    ppermute x1, waiting for transfers between devices, on_device(): taken = lax.ppermute(give, 'bc', [(i, i ^ 1) for i in range(groups)])  1.33 us
  transfers between devices with their start and end apart: 9, of which 4 were waited for; matrix products, arithmetic and copies ran while one was open for 0% of the time, Pallas kernels for 5%

profile of v2, /device:TPU:0, one launch (start us, length us, event | category | flops | bytes accessed | tf_op | source)
XLA Modules:
  0.0 54.8 jit_solution(265634555356373019)
XLA Ops:
  0.0 3.0 %shard_map.55 = (bf16[8,64,384]{2,1,0:T(8,128)(2,1)}, bf16[128,256]{1,0:T(8,128)(2,1)S(1)}, bf16[128,256]{1,0:T(8,128)(2,1)S(1)}, bf16[128,256]{1,0:T(8,128)(2,1...) custom-call(s32[2,8]{1,0:T(2,128)} %bitcast.7, ...), custom_call_target="tpu_custom_call" | custom-call | flops 268435456 | bytes 1048576 | tf_op jit(solution)/shard_map/pallas_call | solution.py:48
  3.0 19.4 %all_to_all.10.orbital_ref.own_ref = bf16[8,64,384]{2,1,0:T(8,128)(2,1)S(1)} all-to-all(bf16[8,64,384]{2,1,0:T(8,128)(2,1)} %get-tuple-element.17), channel_id=1, replica_groups=mesh['ph'=2,'pl'=4,'bx'=2,'bc'=2] {'ph','pl'}, dimensions={0} | all-to-all | bytes 786432 | tf_op jit(solution)/shard_map/all_to_all | solution.py:358
  22.4 0.0 collective-permute-start
  22.4 1.7 %collective-permute-start.1 = (bf16[128,256]{1,0:T(8,128)(2,1)S(1)}, bf16[128,256]{1,0:T(8,128)(2,1)S(1)}, u32[]{:S(2)}, u32[]{:S(2)}) collective-permute-start(bf16[128,256]{1,0:T(8,128)(2,1)S(1)} %get-tuple-element.20), channel_id=1, source_target_pairs={{0,14},{1,15},{2,12},{3,13},{4,10},{5,11},{6,8},{7,9},{8,6},{9,7},... | collective-permute-start | bytes 196616 | tf_op jit(solution)/shard_map/ppermute | solution.py:365
  24.0 1.8 %collective-permute-start.2 = (bf16[128,256]{1,0:T(8,128)(2,1)S(1)}, bf16[128,256]{1,0:T(8,128)(2,1)S(1)}, u32[]{:S(2)}, u32[]{:S(2)}) collective-permute-start(bf16[128,256]{1,0:T(8,128)(2,1)S(1)} %get-tuple-element.21), channel_id=1, source_target_pairs={{0,10},{1,7},{2,8},{3,5},{4,14},{5,3},{6,12},{7,1},{8,2},{9,15},{1... | collective-permute-start | bytes 196616 | tf_op jit(solution)/shard_map/ppermute | solution.py:365
  25.8 1.3 %collective-permute-start.3 = (bf16[128,256]{1,0:T(8,128)(2,1)S(1)}, bf16[128,256]{1,0:T(8,128)(2,1)S(1)}, u32[]{:S(2)}, u32[]{:S(2)}) collective-permute-start(bf16[128,256]{1,0:T(8,128)(2,1)S(1)} %get-tuple-element.22), channel_id=1, source_target_pairs={{0,12},{1,11},{2,14},{3,9},{4,8},{5,15},{6,10},{7,13},{8,4},{9,3},... | collective-permute-start | bytes 196616 | tf_op jit(solution)/shard_map/ppermute | solution.py:365
  27.1 1.1 %collective-permute-start.4 = (bf16[128,256]{1,0:T(8,128)(2,1)S(1)}, bf16[128,256]{1,0:T(8,128)(2,1)S(1)}, u32[]{:S(2)}, u32[]{:S(2)}) collective-permute-start(bf16[128,256]{1,0:T(8,128)(2,1)S(1)} %get-tuple-element.23), channel_id=1, source_target_pairs={{0,8},{1,3},{2,10},{3,1},{4,12},{5,7},{6,14},{7,5},{8,0},{9,11},{1... | collective-permute-start | bytes 196616 | tf_op jit(solution)/shard_map/ppermute | solution.py:365
  28.2 1.5 %shard_map.56._ = bf16[2,1024,512]{2,1,0:T(8,128)(2,1)S(1)} custom-call(bf16[8,64,384]{2,1,0:T(8,128)(2,1)S(1)} %all_to_all.10.orbital_ref.own_ref, bf16[2,1024,512]{2,1,0:T(8,128)(2,1)S(1)} %get-tuple-element.18._), custom_call_target="tpu_custom_call", output_to_operand_aliasing={{}: (1, {})} | custom-call | flops 1073741824 | bytes 1048576 | tf_op jit(solution)/shard_map/pallas_call | solution.py:48
  29.7 0.0 collective-permute-done.1.refs_1_
  29.7 2.1 %collective-permute-start.5 = (bf16[128,256]{1,0:T(8,128)(2,1)S(1)}, bf16[128,256]{1,0:T(8,128)(2,1)S(1)}, u32[]{:S(2)}, u32[]{:S(2)}) collective-permute-start(bf16[128,256]{1,0:T(8,128)(2,1)S(1)} %get-tuple-element.24), channel_id=1, source_target_pairs={{0,6},{1,13},{2,4},{3,15},{4,2},{5,9},{6,0},{7,11},{8,14},{9,5},{1... | collective-permute-start | bytes 196616 | tf_op jit(solution)/shard_map/ppermute | solution.py:365
  31.8 0.0 collective-permute-done.2.refs_2_
  31.8 0.5 collective-permute-start.6
  32.3 0.0 collective-permute-done.orbital_ref.other_ref
  32.3 0.9 %collective-permute-start.7 = (bf16[128,256]{1,0:T(8,128)(2,1)S(1)}, bf16[128,256]{1,0:T(8,128)(2,1)S(1)}, u32[]{:S(2)}, u32[]{:S(2)}) collective-permute-start(bf16[128,256]{1,0:T(8,128)(2,1)S(1)} %get-tuple-element.26), channel_id=1, source_target_pairs={{0,4},{1,9},{2,6},{3,11},{4,0},{5,13},{6,2},{7,15},{8,12},{9,1},{1... | collective-permute-start | bytes 196616 | tf_op jit(solution)/shard_map/ppermute | solution.py:365
  33.3 1.5 %shard_map.57.waves_ref = bf16[2,1024,512]{2,1,0:T(8,128)(2,1)S(1)} custom-call(bf16[8,64,384]{2,1,0:T(8,128)(2,1)S(1)} %collective-permute-done.orbital_ref.other_ref, bf16[2,1024,512]{2,1,0:T(8,128)(2,1)S(1)} %shard_map.56._), custom_call_target="tpu_custom_call", output_to_operand_aliasing={{}: (1, {})} | custom-call | flops 1073741824 | bytes 1048576 | tf_op jit(solution)/shard_map/pallas_call | solution.py:48
  34.7 0.0 collective-permute-done.3.refs_3_
  34.7 0.0 collective-permute-done.4.refs_4_
  34.7 0.2 collective-permute-done.5.refs_5_
  35.0 1.1 %collective-permute-done.6.refs_6_ = bf16[128,256]{1,0:T(8,128)(2,1)S(1)} collective-permute-done((bf16[128,256]{1,0:T(8,128)(2,1)S(1)}, bf16[128,256]{1,0:T(8,128)(2,1)S(1)}, u32[]{:S(2)}, u32[]{:S(2)}) %collective-permute-start.6) | collective-permute-done | bytes 65568 | tf_op jit(solution)/shard_map/ppermute | solution.py:365
  36.0 0.5 collective-permute-done.7.refs_7_
  36.6 0.0 copy-start
  36.6 3.8 %shard_map.58 = (bf16[16,2,16,128]{3,2,1,0:T(8,128)(2,1)S(1)}, bf16[16,2,16,128]{3,2,1,0:T(8,128)(2,1)S(1)}) custom-call(bf16[8,64,384]{2,1,0:T(8,128)(2,1)S(1)} %all_to_all.10.orbital_ref.own_ref, bf16[8,64,384]{2,1,0:T(8,128)(2,1)S(1)} %collective-permute-done.orbital_ref.other_ref, bf16[2,1024,512]{2,1,0:T(8,128)(2,1)S(1)} %shard_map.57.waves_ref, ...), custom_call_target="tpu_custom_call" | custom-call | flops 4831838208 | bytes 1048576 | tf_op jit(solution)/shard_map/pallas_call | solution.py:48
  40.4 0.1 collective-permute-start.8
  40.5 1.3 %collective-permute-done.8 = bf16[16,2,16,128]{3,2,1,0:T(8,128)(2,1)S(1)} collective-permute-done((bf16[16,2,16,128]{3,2,1,0:T(8,128)(2,1)S(1)}, bf16[16,2,16,128]{3,2,1,0:T(8,128)(2,1)S(1)}, u32[]{:S(2)}, u32[]{:S(2)}) %collective-permute-start.8) | collective-permute-done | bytes 131104 | tf_op jit(solution)/shard_map/ppermute | solution.py:412
  41.9 11.6 %all_to_all.11 = bf16[16,2,16,128]{3,2,1,0:T(8,128)(2,1)S(1)} all-to-all(bf16[16,2,16,128]{3,2,1,0:T(8,128)(2,1)S(1)} %add_convert_fusion), channel_id=1, replica_groups=mesh['ph'=2,'pl'=4,'bx'=2,'bc'=2] {'ph','pl','bx'}, dimensions={0} | all-to-all | bytes 262144 | tf_op jit(solution)/shard_map/all_to_all | solution.py:417
  53.5 0.0 copy-done
  53.5 1.3 %shard_map.59 = f32[23,16,128]{2,1,0:T(8,128)} custom-call(s32[2,8]{1,0:T(2,128)S(1)} %bitcast.8, bf16[2,4,2,2,16,128]{5,4,3,2,1,0:T(8,128)(2,1)S(1)} %bitcast.6), custom_call_target="tpu_custom_call" | custom-call | bytes 1048576 | tf_op jit(solution)/shard_map/pallas_call | solution.py:48
  (1 shorter events, 0.0 us)
Async XLA Ops:
  22.4 10.0 %collective-permute-start = (bf16[8,64,384]{2,1,0:T(8,128)(2,1)S(1)}, bf16[8,64,384]{2,1,0:T(8,128)(2,1)S(1)}, u32[]{:S(2)}, u32[]{:S(2)}) collective-permute-start(bf16[8,64,384]{2,1,0:T(8,128)(2,1)S(1)} %all_to_all.10.orbital_ref.own_ref), channel_id=1, source_target_pairs={{0,1},{1,0},{2,3},{3,2},{4,5},{5,4},{6,7},{7,6},{8,9},{9,8},{10,11... | collective-permute-start | bytes 1179656 | tf_op jit(solution)/shard_map/ppermute | solution.py:368
  22.4 7.3 %collective-permute-start.1 = (bf16[128,256]{1,0:T(8,128)(2,1)S(1)}, bf16[128,256]{1,0:T(8,128)(2,1)S(1)}, u32[]{:S(2)}, u32[]{:S(2)}) collective-permute-start(bf16[128,256]{1,0:T(8,128)(2,1)S(1)} %get-tuple-element.20), channel_id=1, source_target_pairs={{0,14},{1,15},{2,12},{3,13},{4,10},{5,11},{6,8},{7,9},{8,6},{9,7},... | collective-permute-start | bytes 196616 | tf_op jit(solution)/shard_map/ppermute | solution.py:365
  24.0 7.7 %collective-permute-start.2 = (bf16[128,256]{1,0:T(8,128)(2,1)S(1)}, bf16[128,256]{1,0:T(8,128)(2,1)S(1)}, u32[]{:S(2)}, u32[]{:S(2)}) collective-permute-start(bf16[128,256]{1,0:T(8,128)(2,1)S(1)} %get-tuple-element.21), channel_id=1, source_target_pairs={{0,10},{1,7},{2,8},{3,5},{4,14},{5,3},{6,12},{7,1},{8,2},{9,15},{1... | collective-permute-start | bytes 196616 | tf_op jit(solution)/shard_map/ppermute | solution.py:365
  25.8 8.9 %collective-permute-start.3 = (bf16[128,256]{1,0:T(8,128)(2,1)S(1)}, bf16[128,256]{1,0:T(8,128)(2,1)S(1)}, u32[]{:S(2)}, u32[]{:S(2)}) collective-permute-start(bf16[128,256]{1,0:T(8,128)(2,1)S(1)} %get-tuple-element.22), channel_id=1, source_target_pairs={{0,12},{1,11},{2,14},{3,9},{4,8},{5,15},{6,10},{7,13},{8,4},{9,3},... | collective-permute-start | bytes 196616 | tf_op jit(solution)/shard_map/ppermute | solution.py:365
  27.1 7.6 %collective-permute-start.4 = (bf16[128,256]{1,0:T(8,128)(2,1)S(1)}, bf16[128,256]{1,0:T(8,128)(2,1)S(1)}, u32[]{:S(2)}, u32[]{:S(2)}) collective-permute-start(bf16[128,256]{1,0:T(8,128)(2,1)S(1)} %get-tuple-element.23), channel_id=1, source_target_pairs={{0,8},{1,3},{2,10},{3,1},{4,12},{5,7},{6,14},{7,5},{8,0},{9,11},{1... | collective-permute-start | bytes 196616 | tf_op jit(solution)/shard_map/ppermute | solution.py:365
  29.7 5.3 %collective-permute-start.5 = (bf16[128,256]{1,0:T(8,128)(2,1)S(1)}, bf16[128,256]{1,0:T(8,128)(2,1)S(1)}, u32[]{:S(2)}, u32[]{:S(2)}) collective-permute-start(bf16[128,256]{1,0:T(8,128)(2,1)S(1)} %get-tuple-element.24), channel_id=1, source_target_pairs={{0,6},{1,13},{2,4},{3,15},{4,2},{5,9},{6,0},{7,11},{8,14},{9,5},{1... | collective-permute-start | bytes 196616 | tf_op jit(solution)/shard_map/ppermute | solution.py:365
  31.8 4.3 %collective-permute-start.6 = (bf16[128,256]{1,0:T(8,128)(2,1)S(1)}, bf16[128,256]{1,0:T(8,128)(2,1)S(1)}, u32[]{:S(2)}, u32[]{:S(2)}) collective-permute-start(bf16[128,256]{1,0:T(8,128)(2,1)S(1)} %get-tuple-element.25), channel_id=1, source_target_pairs={{0,2},{1,5},{2,0},{3,7},{4,6},{5,1},{6,4},{7,3},{8,10},{9,13},{10,... | collective-permute-start | bytes 196616 | tf_op jit(solution)/shard_map/ppermute | solution.py:365
  32.3 4.3 %collective-permute-start.7 = (bf16[128,256]{1,0:T(8,128)(2,1)S(1)}, bf16[128,256]{1,0:T(8,128)(2,1)S(1)}, u32[]{:S(2)}, u32[]{:S(2)}) collective-permute-start(bf16[128,256]{1,0:T(8,128)(2,1)S(1)} %get-tuple-element.26), channel_id=1, source_target_pairs={{0,4},{1,9},{2,6},{3,11},{4,0},{5,13},{6,2},{7,15},{8,12},{9,1},{1... | collective-permute-start | bytes 196616 | tf_op jit(solution)/shard_map/ppermute | solution.py:365
  36.6 16.9 %copy-start = (s32[8,2]{0,1:T(2,128)S(1)}, s32[8,2]{0,1:T(2,128)}, u32[]{:S(2)}) copy-start(s32[8,2]{0,1:T(2,128)} %param.8) | copy-start | bytes 196
  40.4 1.4 %collective-permute-start.8 = (bf16[16,2,16,128]{3,2,1,0:T(8,128)(2,1)S(1)}, bf16[16,2,16,128]{3,2,1,0:T(8,128)(2,1)S(1)}, u32[]{:S(2)}, u32[]{:S(2)}) collective-permute-start(bf16[16,2,16,128]{3,2,1,0:T(8,128)(2,1)S(1)} %get-tuple-element.28), channel_id=1, source_target_pairs={{0,1},{1,0},{2,3},{3,2},{4,5},{5,4},{6,7},{7,6},{8,9},{9,8},{10,11... | collective-permute-start | bytes 393224 | tf_op jit(solution)/shard_map/ppermute | solution.py:412
